TPU v7x, 128 devices: a whole 4x4x4 slice. The times are simulated.
128 devices in a mesh: ctx: 32 (over x, z, core), head: 4 (over y).
Axes of the slice: x: 4, y: 4, z: 4, core: 2. Of those that a mesh axis runs over, the one named last changes fastest.
Arguments:
- query_raw: bfloat16 [32768, 2048], P('ctx', 'head'), may hold values from -6 to 6
- key_raw: bfloat16 [32768, 2048], P('ctx', 'head'), may hold values from -6 to 6
- value_raw: bfloat16 [32768, 4096], P('ctx', 'head'), may hold values from -6 to 6
- gate_branch: bfloat16 [32768, 4096], P('ctx', 'head'), may hold values from -6 to 6
- gate_code: int32 [32768, 32], P('ctx', 'head'), may hold values from 0 to 1000
- beta_code: int32 [32768, 32], P('ctx', 'head'), may hold values from 0 to 1000
- conv_query: bfloat16 [4, 2048], P(None, 'head'), may hold values from -3 to 3
- conv_key: bfloat16 [4, 2048], P(None, 'head'), may hold values from -3 to 3
- conv_value: bfloat16 [4, 4096], P(None, 'head'), may hold values from -3 to 3
- norm_gain: float32 [128], replicated, may hold values from 0.1 to 1.9
- out_weight: bfloat16 [4096, 2048], P('head'), may hold values from -0.09375 to 0.09375
Outputs:
- layer_out: bfloat16 [32768, 2048], P(('ctx', 'head'))
All inputs are finite; a program needn't handle non-finite values.
Results may differ from a plain program's by a relative error of at most 0.002.
The roundings to bfloat16 on the way count: a program that leaves them out, or rounds other values in their place, can miss the bound.
Values may be sent and summed in bfloat16 or wider, within the bound.
No kernel may reach another device: no remote copies, remote signals or barrier semaphores. Data moves between devices by JAX's collectives and lax.ppermute only.
A program may use at most 128 MiB of HBM per device.

v0:
```python
import jax
import jax.numpy as jnp
from jax import lax
from jax.sharding import PartitionSpec as P

HEAD_DIM = 128
KERNEL = 4
BLOCK = 64


EXACT = lax.Precision.HIGHEST


def passed_along(block, axis, distance):
    devices = range(lax.axis_size(axis))
    route = [(i - distance, i) for i in devices if i - distance in devices]
    return lax.ppermute(block, axis, route)


def causal_conv(earlier, current, weights):
    length = current.shape[0]
    extended = jnp.concatenate([earlier, current], 0).astype(jnp.float32)
    running = jnp.zeros(current.shape, jnp.float32)
    for offset in range(KERNEL):
        running = running + weights[offset].astype(jnp.float32) * extended[offset : offset + length]
    return jax.nn.silu(running)


def unit_rows(values):
    return values * lax.rsqrt(jnp.sum(values * values, -1, keepdims=True) + 1e-06)


def neumann_inverse(strict_part):
    length = strict_part.shape[-1]
    identity = jnp.eye(length, dtype=jnp.float32)
    result = identity - strict_part
    powered = strict_part
    covered = 2
    while covered < length:
        powered = jnp.matmul(powered, powered, precision=EXACT)
        result = jnp.matmul(result, identity + powered, precision=EXACT)
        covered = covered * 2
    return result


def prepare(queries, key_rows, value_rows, log_gate, strength):
    length = queries.shape[-2]
    cumulated = jnp.cumsum(log_gate, axis=-1)
    gap_log = cumulated[..., :, None] - cumulated[..., None, :]
    row_ids = lax.broadcasted_iota(jnp.int32, (length, length), 0)
    col_ids = lax.broadcasted_iota(jnp.int32, (length, length), 1)
    causal_mask = row_ids >= col_ids
    strict_mask = row_ids > col_ids
    decays = jnp.exp(jnp.where(causal_mask, gap_log, 0.0))
    key_dots = jnp.einsum("...id,...jd->...ij", key_rows, key_rows, precision=EXACT)
    strict_part = jnp.where(strict_mask, strength[..., :, None] * key_dots * decays, 0.0)
    inverse = neumann_inverse(strict_part)
    gammas = jnp.exp(cumulated)
    wy_keys = jnp.einsum(
        "...ij,...jd->...id", inverse, (strength * gammas)[..., None] * key_rows, precision=EXACT
    )
    wy_values = jnp.einsum(
        "...ij,...jd->...id", inverse, strength[..., None] * value_rows, precision=EXACT
    )
    query_dots = jnp.einsum("...id,...jd->...ij", queries, key_rows, precision=EXACT)
    mixing = jnp.where(causal_mask, query_dots * decays, 0.0)
    key_tails = jnp.exp(cumulated[..., -1:] - cumulated)[..., None] * key_rows
    block_decay = jnp.exp(cumulated[..., -1])
    return (gammas, mixing, wy_keys, wy_values, key_tails, block_decay)


def gated_norm(emitted, branch, gain_vector):
    scaled = (
        emitted * lax.rsqrt(jnp.mean(emitted * emitted, -1, keepdims=True) + 1e-06) * gain_vector
    )
    gating = jax.nn.silu(branch.astype(jnp.float32)).reshape(emitted.shape)
    return (scaled * gating).reshape(emitted.shape[0], -1).astype(jnp.bfloat16)


def shards(
    query_raw,
    key_raw,
    value_raw,
    gate_branch,
    gate_code,
    beta_code,
    conv_query,
    conv_key,
    conv_value,
    norm_gain,
    out_weight,
):
    tok_rows = query_raw.shape[0]
    key_heads = query_raw.shape[1] // HEAD_DIM
    value_heads = value_raw.shape[1] // HEAD_DIM
    group_ratio = value_heads // key_heads
    blocks = tok_rows // BLOCK
    margin = KERNEL - 1
    rim_rows = passed_along(
        (
            query_raw[tok_rows - margin :],
            key_raw[tok_rows - margin :],
            value_raw[tok_rows - margin :],
        ),
        "ctx",
        1,
    )
    query_conv = causal_conv(rim_rows[0], query_raw, conv_query)
    key_conv = causal_conv(rim_rows[1], key_raw, conv_key)
    value_conv = causal_conv(rim_rows[2], value_raw, conv_value)
    queries = unit_rows(query_conv.reshape(blocks, BLOCK, key_heads, HEAD_DIM)) * HEAD_DIM ** (-0.5)
    key_rows = unit_rows(key_conv.reshape(blocks, BLOCK, key_heads, HEAD_DIM))
    queries = jnp.repeat(queries, group_ratio, axis=2).transpose(0, 2, 1, 3)
    key_rows = jnp.repeat(key_rows, group_ratio, axis=2).transpose(0, 2, 1, 3)
    value_rows = value_conv.reshape(blocks, BLOCK, value_heads, HEAD_DIM).transpose(0, 2, 1, 3)
    log_gate = (
        jnp.log1p(-1e-06 * gate_code.astype(jnp.float32))
        .reshape(blocks, BLOCK, value_heads)
        .transpose(0, 2, 1)
    )
    strength = (
        (beta_code.astype(jnp.float32) / 1000.0)
        .reshape(blocks, BLOCK, value_heads)
        .transpose(0, 2, 1)
    )
    gammas, mixing, wy_keys, wy_values, key_tails, block_decay = prepare(
        queries, key_rows, value_rows, log_gate, strength
    )
    identity = jnp.eye(HEAD_DIM, dtype=jnp.float32)
    block_maps = block_decay[..., None, None] * identity - jnp.einsum(
        "nhjd,nhje->nhde", key_tails, wy_keys, precision=EXACT
    )
    block_sums = jnp.einsum("nhjd,nhje->nhde", key_tails, wy_values, precision=EXACT)

    def compose(loop_carry, pieces):
        acc_map, acc_sum = loop_carry
        step_map, step_sum = pieces
        return (
            (
                jnp.matmul(step_map, acc_map, precision=EXACT),
                jnp.matmul(step_map, acc_sum, precision=EXACT) + step_sum,
            ),
            None,
        )

    start_map = jnp.broadcast_to(identity, (value_heads, HEAD_DIM, HEAD_DIM))
    zero_state = jnp.zeros((value_heads, HEAD_DIM, HEAD_DIM), jnp.float32)
    (dev_map, dev_sum), _ = lax.scan(compose, (start_map, zero_state), (block_maps, block_sums))
    emit_rows = gammas[..., None] * queries - jnp.matmul(mixing, wy_keys, precision=EXACT)
    base_rows = jnp.matmul(mixing, wy_values, precision=EXACT)
    position = lax.axis_index("ctx")

    def relay_hop(hop_index, received):
        outgoing = jnp.matmul(dev_map, received, precision=EXACT) + dev_sum
        arrived = passed_along(outgoing, "ctx", 1)
        return jnp.where(position == hop_index, arrived, received)

    incoming = lax.fori_loop(1, lax.axis_size("ctx"), relay_hop, zero_state)

    def advance(carried, pieces):
        step_map, step_sum, emit_block, base_block = pieces
        emitted = base_block + jnp.matmul(emit_block, carried, precision=EXACT)
        return (jnp.matmul(step_map, carried, precision=EXACT) + step_sum, emitted)

    _, emitted = lax.scan(advance, incoming, (block_maps, block_sums, emit_rows, base_rows))
    emitted = emitted.transpose(0, 2, 1, 3).reshape(tok_rows, value_heads, HEAD_DIM)
    normed = gated_norm(emitted, gate_branch, norm_gain)
    return lax.psum_scatter(
        jnp.dot(normed, out_weight, preferred_element_type=jnp.float32),
        "head",
        scatter_dimension=0,
        tiled=True,
    ).astype(jnp.bfloat16)


def solution(mesh):
    return jax.shard_map(
        shards,
        mesh=mesh,
        in_specs=(
            P("ctx", "head"),
            P("ctx", "head"),
            P("ctx", "head"),
            P("ctx", "head"),
            P("ctx", "head"),
            P("ctx", "head"),
            P(None, "head"),
            P(None, "head"),
            P(None, "head"),
            P(),
            P("head", None),
        ),
        out_specs=P(("ctx", "head"), None),
        check_vma=False,
    )
```

profile of v0, /device:TPU:1, one launch (start us, length us, event | category | flops | bytes accessed | tf_op | source)
XLA Modules:
  0.0 837.7 jit_solution(3929203638494448519)
XLA Ops:
  40.6 7.0 fusion.104
  47.6 8.5 %fusion.55 = f32[16,8,64,64]{3,2,1,0:T(8,128)S(1)} fusion(f32[16,8,64,64]{3,2,1,0:T(8,128)S(1)} %fusion.104, f32[16,8,64]{2,1,0:T(8,128)S(1)} %reduce_window_sum.11, f32[16,8,64]{2,1,0:T(8,128)S(1)} %bitcast.146, pred[64,64]{1,0:T(8,128)(4,1)S(1)} %get-tuple-element.253, pred[64,64]{1,0:T(8,128)(4,1)S(1)} %get-tuple-element.254), kind=kOutput, calls=%fused_computation.73 | convolution fusion | flops 405274624 | bytes 4268032 | tf_op jit(solution)/shard_map/dot_general | solution.py:40
  61.6 7.0 fusion.43
  113.5 6.8 fusion.109
  129.9 7.5 multiply_subtract_fusion.1
  137.4 17.7 %multiply_subtract_fusion = f32[16,8,128,128]{3,2,1,0:T(8,128)} fusion(f32[128,128]{1,0:T(8,128)S(1)} %fusion.95, f32[16,8]{1,0:T(8,128)S(1)} %copy.39, f32[16,8,64,128]{3,2,1,0:T(8,128)S(1)} %fusion.33, f32[16,8,64,128]{3,2,1,0:T(8,128)S(1)} %bitcast.137, f32[16,8,64]{2,1,0:T(8,128)S(1)} %get-tuple-element.240), kind=kOutput, calls=%fused_computation.28 | convolution fusion | flops 1615855616 | bytes 16876032 | tf_op jit(solution)/shard_map/nhjd,nhje->nhde/dot_general | solution.py:130
  164.4 6.7 fusion.54
  171.1 16.9 %fusion.47 = f32[16,8,128,128]{3,2,1,0:T(8,128)} fusion(f32[16,8,64,128]{3,2,1,0:T(8,128)S(1)} %fusion.31, f32[16,8,64,128]{3,2,1,0:T(8,128)S(1)} %bitcast.138, f32[16,8,64]{2,1,0:T(8,128)S(1)} %get-tuple-element.240), kind=kOutput, calls=%fused_computation.67 | convolution fusion | flops 1611661312 | bytes 16809984 | tf_op jit(solution)/shard_map/nhjd,nhje->nhde/dot_general | solution.py:133
  188.0 58.9 %while.40 = (s32[]{:T(128)}, f32[8,128,128]{2,1,0:T(8,128)S(1)}, f32[8,128,128]{2,1,0:T(8,128)S(1)}, f32[16,8,128,128]{3,2,1,0:T(8,128)}, f32[16,8,128,128]{3,2,1,0:T(8,128)}, /*index=5*/s32[]{:T(128)}, s32[]{:T(128)}) while((s32[]{:T(128)}, f32[8,128,128]{2,1,0:T(8,128)S(1)}, f32[8,128,128]{2,1,0:T(8,128)S(1)}, ...), condition=%wide.region_3.4_spmd.clone, body=%wide.region_2.3_spmd.clone.sunk | while | flops 402915328 | bytes 5768791 | solution.py:148
  246.9 374.7 %while.41 = (s32[]{:T(128)}, f32[8,128,128]{2,1,0:T(8,128)S(1)}, s32[]{:T(128)}, f32[8,128,128]{2,1,0:T(8,128)S(1)}, f32[8,128,128]{2,1,0:T(8,128)S(1)}, /*index=5*/s32[]{:T(128)}, s32[]{:T(128)}) while((s32[]{:T(128)}, f32[8,128,128]{2,1,0:T(8,128)S(1)}, s32[]{:T(128)}, f32[8,128,128]{2,1,0:T(8,128)S(1)}, ...), condition=%wide.region_5.6_spmd.clone, body=%wide.region_4.5_spmd.clone.sunk | while | flops 201850880 | bytes 5767306 | solution.py:158
  461.0 6.5 collective-permute-start
  474.5 6.5 collective-permute-start
  487.9 6.5 collective-permute-start
  501.3 6.5 collective-permute-start
  514.8 6.5 collective-permute-start
  528.2 6.5 collective-permute-start
  541.7 6.5 collective-permute-start
  555.1 6.5 collective-permute-start
  568.5 6.5 collective-permute-start
  582.0 6.5 collective-permute-start
  608.8 6.5 collective-permute-start
  621.6 68.2 %while.39 = (s32[]{:T(128)}, f32[8,128,128]{2,1,0:T(8,128)S(1)}, f32[16,8,64,128]{3,2,1,0:T(8,128)}, f32[16,8,128,128]{3,2,1,0:T(8,128)}, f32[16,8,128,128]{3,2,...) while((s32[]{:T(128)}, f32[8,128,128]{2,1,0:T(8,128)S(1)}, ...), condition=%wide.region_8.9_spmd, body=%wide.region_7.8_spmd.sunk | while | flops 302186496 | bytes 4458581 | solution.py:165
  701.2 7.5 fusion.56
  708.7 119.3 %reduce-scatter.2.cloned.1.call-done = f32[256,2048]{1,0:T(8,128)} async-done(((f32[1024,2048]{1,0:T(8,128)}), f32[256,2048]{1,0:T(8,128)}) %reduce-scatter.2.cloned.1.call-update) | async-done | bytes 2097168 | tf_op jit(solution)/shard_map/reduce_scatter | solution.py:168
  (327 shorter events, 544.5 us)
Async XLA Ops:
  6.5 821.4 %reduce-scatter.2.cloned.1.call-start = ((), (), s32[]{:S(2)}) async-start(), calls=%async_computation.1 | async-start | bytes 10485760 | tf_op jit(solution)/shard_map/reduce_scatter | solution.py:168
  7.3 23.6 %collective-permute-start.1 = (bf16[3,512]{1,0:T(4,128)(2,1)S(1)}, bf16[3,512]{1,0:T(4,128)(2,1)S(1)}, u32[]{:S(2)}, u32[]{:S(2)}) collective-permute-start(bf16[3,512]{1,0:T(4,128)(2,1)S(1)} %slice.87), channel_id=1, source_target_pairs={{0,4},{4,8},{8,12},{12,16},{16,20},{20,24},{24,28},{28,32},{32,36}... | collective-permute-start | bytes 9224 | tf_op jit(solution)/shard_map/ppermute | solution.py:17
  13.5 88.9 %collective-permute-start.3 = (bf16[3,512]{1,0:T(4,128)(2,1)}, bf16[3,512]{1,0:T(4,128)(2,1)}, u32[]{:S(2)}, u32[]{:S(2)}) collective-permute-start(bf16[3,512]{1,0:T(4,128)(2,1)} %slice.105), channel_id=1, source_target_pairs={{0,4},{4,8},{8,12},{12,16},{16,20},{20,24},{24,28},{28,32},{32,36}... | collective-permute-start | bytes 9224 | tf_op jit(solution)/shard_map/ppermute | solution.py:17
  16.7 138.4 %collective-permute-start.2 = (bf16[3,1024]{1,0:T(4,128)(2,1)}, bf16[3,1024]{1,0:T(4,128)(2,1)S(1)}, u32[]{:S(2)}, u32[]{:S(2)}) collective-permute-start(bf16[3,1024]{1,0:T(4,128)(2,1)} %slice.96), channel_id=1, source_target_pairs={{0,4},{4,8},{8,12},{12,16},{16,20},{20,24},{24,28},{28,32},{32,36}... | collective-permute-start | bytes 18440 | tf_op jit(solution)/shard_map/ppermute | solution.py:17
  267.8 10.5 %collective-permute-start = (f32[8,128,128]{2,1,0:T(8,128)S(1)}, f32[8,128,128]{2,1,0:T(8,128)S(1)}, u32[]{:S(2)}, u32[]{:S(2)}) collective-permute-start(f32[8,128,128]{2,1,0:T(8,128)S(1)} %convolution_add_fusion.9), channel_id=1, source_target_pairs={{0,4},{4,8},{8,12},{12,16},{16,20},{20,24},{24,28},{28,32},{32,36}... | collective-permute-start | bytes 1572872 | tf_op jit(solution)/shard_map/while/body/eval_jaxpr/ppermute | solution.py:17
  279.1 10.5 %collective-permute-start = (f32[8,128,128]{2,1,0:T(8,128)S(1)}, f32[8,128,128]{2,1,0:T(8,128)S(1)}, u32[]{:S(2)}, u32[]{:S(2)}) collective-permute-start(f32[8,128,128]{2,1,0:T(8,128)S(1)} %convolution_add_fusion.9), channel_id=1, source_target_pairs={{0,4},{4,8},{8,12},{12,16},{16,20},{20,24},{24,28},{28,32},{32,36}... | collective-permute-start | bytes 1572872 | tf_op jit(solution)/shard_map/while/body/eval_jaxpr/ppermute | solution.py:17
  324.4 10.5 %collective-permute-start = (f32[8,128,128]{2,1,0:T(8,128)S(1)}, f32[8,128,128]{2,1,0:T(8,128)S(1)}, u32[]{:S(2)}, u32[]{:S(2)}) collective-permute-start(f32[8,128,128]{2,1,0:T(8,128)S(1)} %convolution_add_fusion.9), channel_id=1, source_target_pairs={{0,4},{4,8},{8,12},{12,16},{16,20},{20,24},{24,28},{28,32},{32,36}... | collective-permute-start | bytes 1572872 | tf_op jit(solution)/shard_map/while/body/eval_jaxpr/ppermute | solution.py:17
  335.7 10.5 %collective-permute-start = (f32[8,128,128]{2,1,0:T(8,128)S(1)}, f32[8,128,128]{2,1,0:T(8,128)S(1)}, u32[]{:S(2)}, u32[]{:S(2)}) collective-permute-start(f32[8,128,128]{2,1,0:T(8,128)S(1)} %convolution_add_fusion.9), channel_id=1, source_target_pairs={{0,4},{4,8},{8,12},{12,16},{16,20},{20,24},{24,28},{28,32},{32,36}... | collective-permute-start | bytes 1572872 | tf_op jit(solution)/shard_map/while/body/eval_jaxpr/ppermute | solution.py:17
  381.1 10.5 %collective-permute-start = (f32[8,128,128]{2,1,0:T(8,128)S(1)}, f32[8,128,128]{2,1,0:T(8,128)S(1)}, u32[]{:S(2)}, u32[]{:S(2)}) collective-permute-start(f32[8,128,128]{2,1,0:T(8,128)S(1)} %convolution_add_fusion.9), channel_id=1, source_target_pairs={{0,4},{4,8},{8,12},{12,16},{16,20},{20,24},{24,28},{28,32},{32,36}... | collective-permute-start | bytes 1572872 | tf_op jit(solution)/shard_map/while/body/eval_jaxpr/ppermute | solution.py:17
  392.4 10.5 %collective-permute-start = (f32[8,128,128]{2,1,0:T(8,128)S(1)}, f32[8,128,128]{2,1,0:T(8,128)S(1)}, u32[]{:S(2)}, u32[]{:S(2)}) collective-permute-start(f32[8,128,128]{2,1,0:T(8,128)S(1)} %convolution_add_fusion.9), channel_id=1, source_target_pairs={{0,4},{4,8},{8,12},{12,16},{16,20},{20,24},{24,28},{28,32},{32,36}... | collective-permute-start | bytes 1572872 | tf_op jit(solution)/shard_map/while/body/eval_jaxpr/ppermute | solution.py:17
  437.7 10.5 %collective-permute-start = (f32[8,128,128]{2,1,0:T(8,128)S(1)}, f32[8,128,128]{2,1,0:T(8,128)S(1)}, u32[]{:S(2)}, u32[]{:S(2)}) collective-permute-start(f32[8,128,128]{2,1,0:T(8,128)S(1)} %convolution_add_fusion.9), channel_id=1, source_target_pairs={{0,4},{4,8},{8,12},{12,16},{16,20},{20,24},{24,28},{28,32},{32,36}... | collective-permute-start | bytes 1572872 | tf_op jit(solution)/shard_map/while/body/eval_jaxpr/ppermute | solution.py:17
  449.0 11.2 %collective-permute-start = (f32[8,128,128]{2,1,0:T(8,128)S(1)}, f32[8,128,128]{2,1,0:T(8,128)S(1)}, u32[]{:S(2)}, u32[]{:S(2)}) collective-permute-start(f32[8,128,128]{2,1,0:T(8,128)S(1)} %convolution_add_fusion.9), channel_id=1, source_target_pairs={{0,4},{4,8},{8,12},{12,16},{16,20},{20,24},{24,28},{28,32},{32,36}... | collective-permute-start | bytes 1572872 | tf_op jit(solution)/shard_map/while/body/eval_jaxpr/ppermute | solution.py:17
  461.0 12.6 %collective-permute-start = (f32[8,128,128]{2,1,0:T(8,128)S(1)}, f32[8,128,128]{2,1,0:T(8,128)S(1)}, u32[]{:S(2)}, u32[]{:S(2)}) collective-permute-start(f32[8,128,128]{2,1,0:T(8,128)S(1)} %convolution_add_fusion.9), channel_id=1, source_target_pairs={{0,4},{4,8},{8,12},{12,16},{16,20},{20,24},{24,28},{28,32},{32,36}... | collective-permute-start | bytes 1572872 | tf_op jit(solution)/shard_map/while/body/eval_jaxpr/ppermute | solution.py:17
  474.5 12.6 %collective-permute-start = (f32[8,128,128]{2,1,0:T(8,128)S(1)}, f32[8,128,128]{2,1,0:T(8,128)S(1)}, u32[]{:S(2)}, u32[]{:S(2)}) collective-permute-start(f32[8,128,128]{2,1,0:T(8,128)S(1)} %convolution_add_fusion.9), channel_id=1, source_target_pairs={{0,4},{4,8},{8,12},{12,16},{16,20},{20,24},{24,28},{28,32},{32,36}... | collective-permute-start | bytes 1572872 | tf_op jit(solution)/shard_map/while/body/eval_jaxpr/ppermute | solution.py:17
  487.9 12.6 %collective-permute-start = (f32[8,128,128]{2,1,0:T(8,128)S(1)}, f32[8,128,128]{2,1,0:T(8,128)S(1)}, u32[]{:S(2)}, u32[]{:S(2)}) collective-permute-start(f32[8,128,128]{2,1,0:T(8,128)S(1)} %convolution_add_fusion.9), channel_id=1, source_target_pairs={{0,4},{4,8},{8,12},{12,16},{16,20},{20,24},{24,28},{28,32},{32,36}... | collective-permute-start | bytes 1572872 | tf_op jit(solution)/shard_map/while/body/eval_jaxpr/ppermute | solution.py:17
  501.3 12.6 %collective-permute-start = (f32[8,128,128]{2,1,0:T(8,128)S(1)}, f32[8,128,128]{2,1,0:T(8,128)S(1)}, u32[]{:S(2)}, u32[]{:S(2)}) collective-permute-start(f32[8,128,128]{2,1,0:T(8,128)S(1)} %convolution_add_fusion.9), channel_id=1, source_target_pairs={{0,4},{4,8},{8,12},{12,16},{16,20},{20,24},{24,28},{28,32},{32,36}... | collective-permute-start | bytes 1572872 | tf_op jit(solution)/shard_map/while/body/eval_jaxpr/ppermute | solution.py:17
  514.8 12.6 %collective-permute-start = (f32[8,128,128]{2,1,0:T(8,128)S(1)}, f32[8,128,128]{2,1,0:T(8,128)S(1)}, u32[]{:S(2)}, u32[]{:S(2)}) collective-permute-start(f32[8,128,128]{2,1,0:T(8,128)S(1)} %convolution_add_fusion.9), channel_id=1, source_target_pairs={{0,4},{4,8},{8,12},{12,16},{16,20},{20,24},{24,28},{28,32},{32,36}... | collective-permute-start | bytes 1572872 | tf_op jit(solution)/shard_map/while/body/eval_jaxpr/ppermute | solution.py:17
  528.2 12.6 %collective-permute-start = (f32[8,128,128]{2,1,0:T(8,128)S(1)}, f32[8,128,128]{2,1,0:T(8,128)S(1)}, u32[]{:S(2)}, u32[]{:S(2)}) collective-permute-start(f32[8,128,128]{2,1,0:T(8,128)S(1)} %convolution_add_fusion.9), channel_id=1, source_target_pairs={{0,4},{4,8},{8,12},{12,16},{16,20},{20,24},{24,28},{28,32},{32,36}... | collective-permute-start | bytes 1572872 | tf_op jit(solution)/shard_map/while/body/eval_jaxpr/ppermute | solution.py:17
  541.7 12.6 %collective-permute-start = (f32[8,128,128]{2,1,0:T(8,128)S(1)}, f32[8,128,128]{2,1,0:T(8,128)S(1)}, u32[]{:S(2)}, u32[]{:S(2)}) collective-permute-start(f32[8,128,128]{2,1,0:T(8,128)S(1)} %convolution_add_fusion.9), channel_id=1, source_target_pairs={{0,4},{4,8},{8,12},{12,16},{16,20},{20,24},{24,28},{28,32},{32,36}... | collective-permute-start | bytes 1572872 | tf_op jit(solution)/shard_map/while/body/eval_jaxpr/ppermute | solution.py:17
  555.1 12.6 %collective-permute-start = (f32[8,128,128]{2,1,0:T(8,128)S(1)}, f32[8,128,128]{2,1,0:T(8,128)S(1)}, u32[]{:S(2)}, u32[]{:S(2)}) collective-permute-start(f32[8,128,128]{2,1,0:T(8,128)S(1)} %convolution_add_fusion.9), channel_id=1, source_target_pairs={{0,4},{4,8},{8,12},{12,16},{16,20},{20,24},{24,28},{28,32},{32,36}... | collective-permute-start | bytes 1572872 | tf_op jit(solution)/shard_map/while/body/eval_jaxpr/ppermute | solution.py:17
  568.5 12.6 %collective-permute-start = (f32[8,128,128]{2,1,0:T(8,128)S(1)}, f32[8,128,128]{2,1,0:T(8,128)S(1)}, u32[]{:S(2)}, u32[]{:S(2)}) collective-permute-start(f32[8,128,128]{2,1,0:T(8,128)S(1)} %convolution_add_fusion.9), channel_id=1, source_target_pairs={{0,4},{4,8},{8,12},{12,16},{16,20},{20,24},{24,28},{28,32},{32,36}... | collective-permute-start | bytes 1572872 | tf_op jit(solution)/shard_map/while/body/eval_jaxpr/ppermute | solution.py:17
  582.0 12.6 %collective-permute-start = (f32[8,128,128]{2,1,0:T(8,128)S(1)}, f32[8,128,128]{2,1,0:T(8,128)S(1)}, u32[]{:S(2)}, u32[]{:S(2)}) collective-permute-start(f32[8,128,128]{2,1,0:T(8,128)S(1)} %convolution_add_fusion.9), channel_id=1, source_target_pairs={{0,4},{4,8},{8,12},{12,16},{16,20},{20,24},{24,28},{28,32},{32,36}... | collective-permute-start | bytes 1572872 | tf_op jit(solution)/shard_map/while/body/eval_jaxpr/ppermute | solution.py:17
  595.4 12.6 %collective-permute-start = (f32[8,128,128]{2,1,0:T(8,128)S(1)}, f32[8,128,128]{2,1,0:T(8,128)S(1)}, u32[]{:S(2)}, u32[]{:S(2)}) collective-permute-start(f32[8,128,128]{2,1,0:T(8,128)S(1)} %convolution_add_fusion.9), channel_id=1, source_target_pairs={{0,4},{4,8},{8,12},{12,16},{16,20},{20,24},{24,28},{28,32},{32,36}... | collective-permute-start | bytes 1572872 | tf_op jit(solution)/shard_map/while/body/eval_jaxpr/ppermute | solution.py:17
  608.8 12.6 %collective-permute-start = (f32[8,128,128]{2,1,0:T(8,128)S(1)}, f32[8,128,128]{2,1,0:T(8,128)S(1)}, u32[]{:S(2)}, u32[]{:S(2)}) collective-permute-start(f32[8,128,128]{2,1,0:T(8,128)S(1)} %convolution_add_fusion.9), channel_id=1, source_target_pairs={{0,4},{4,8},{8,12},{12,16},{16,20},{20,24},{24,28},{28,32},{32,36}... | collective-permute-start | bytes 1572872 | tf_op jit(solution)/shard_map/while/body/eval_jaxpr/ppermute | solution.py:17
  (27 other events, 347.2 us)
Sparse Core Ops, SparseCore 0:
  708.8 119.0 reduce-scatter.1
where the time goes:
time: 845 us; the launch traced here: 838 us
  waiting for transfers between devices  308 us (36%)
  matrix products  283 us (33%)
  starting transfers between devices  170 us (20%)
  other arithmetic  36.6 us (4%)
  local copies, waits for them, and re-layouts  22.5 us (3%)
  between operations  14.1 us (2%)
    ppermute x34, waiting for transfers between devices, passed_along(): return lax.ppermute(block, axis, route)  189 us
    ppermute x34, starting transfers between devices, passed_along(): return lax.ppermute(block, axis, route)  170 us
    reduce_scatter x1, waiting for transfers between devices, shards(): lax.psum_scatter(jnp.dot(normed, out_weight, preferred_element_type=jnp.f...  119 us
    dot_general x16, matrix products, advance(): emitted = base_block + jnp.matmul(emit_block, carried, precision=EXACT)  37.5 us
    dot_general x5, matrix products, neumann_inverse(): powered = jnp.matmul(powered, powered, precision=EXACT)  31.1 us
    dot_general x16, matrix products, compose(): jnp.matmul(step_map, acc_sum, precision=EXACT) + step_sum  29.6 us
    dot_general x16, matrix products, advance(): return (jnp.matmul(step_map, carried, precision=EXACT) + step_sum, emitted)  29.5 us
    dot_general x5, matrix products, neumann_inverse(): result = jnp.matmul(result, identity + powered, precision=EXACT)  28.6 us
  transfers between devices with their start and end apart: 35, of which 32 were waited for; matrix products, arithmetic and copies ran while one was open for 16% of the time, Pallas kernels for 0%

commit v1 on v0

v1 whole, which is shorter than its diff:
```python
import jax, jax.numpy as jnp
from jax import lax
from jax.experimental import pallas as pl
from jax.experimental.pallas import tpu as pltpu
from jax.sharding import PartitionSpec as P

Z_CHIPS, X_CHIPS, CORES = 4, 4, 2

F32, BF16 = jnp.float32, jnp.bfloat16
HD = 128
BLOCK = 64
KERNEL = 4


def split(x):
    hi = x.astype(BF16)
    return hi, (x - hi.astype(F32)).astype(BF16)


def mxu(a, b):
    return jnp.dot(a, b, preferred_element_type=F32)


def cat(parts, axis):
    return jnp.concatenate(parts, axis)


def silu(x):
    return x / (1.0 + jnp.exp(-x))


def pair_rhs(y, left):
    hi, lo = split(y)
    zero = jnp.zeros_like(hi)
    hi = cat([jnp.where(left, hi, zero), jnp.where(left, zero, hi)], 0)
    lo = cat([jnp.where(left, lo, zero), jnp.where(left, zero, lo)], 0)
    row = cat([hi, lo], 1)
    return cat([row, row], 0)


def wide(x):
    return cat(split(x), 1)


def fold(out):
    return out[:, :HD] + out[:, HD:]


def pair_inverse(low, eye, left):
    inv = eye - low
    power = fold(mxu(wide(low), pair_rhs(low, left)))
    covered = 4
    while covered < BLOCK:
        out = fold(mxu(wide(cat([inv, power], 0)), pair_rhs(power, left)))
        inv = inv + out[:BLOCK]
        power = out[BLOCK:]
        covered *= 2
    return inv + fold(mxu(wide(inv), pair_rhs(power, left)))


def conv(ext, taps):
    acc = None
    for j in range(KERNEL):
        s = KERNEL - 1 - j
        shifted = ext if s == 0 else pltpu.roll(ext, s, 0)
        term = taps[j : j + 1] * shifted[8:]
        acc = term if acc is None else acc + term
    return silu(acc)


def unit(x):
    return x * lax.rsqrt(jnp.sum(x * x, -1, keepdims=True) + 1e-06)


def scan_kernel(q_ref, k_ref, v_ref, gc_ref, bc_ref, halo_ref, cq_ref, ck_ref, cv_ref,
                base_ref, map_ref, fin_ref, state, carry):
    n = pl.program_id(0)
    kh = q_ref.shape[1] // HD
    vh = v_ref.shape[1] // HD
    kw, vw = kh * HD, vh * HD

    @pl.when(n == 0)
    def _():
        carry[...] = halo_ref[...].astype(F32)
        r = lax.broadcasted_iota(jnp.int32, (HD, 2 * HD), 0)
        c = lax.broadcasted_iota(jnp.int32, (HD, 2 * HD), 1)
        start = jnp.where(r + HD == c, 1.0, 0.0).astype(F32)
        for h in range(vh):
            state[h] = start

    rows = lax.broadcasted_iota(jnp.int32, (BLOCK, HD), 0)
    lanes = lax.broadcasted_iota(jnp.int32, (BLOCK, HD), 1)
    left = lanes < BLOCK
    cols = jnp.where(left, lanes, lanes - BLOCK)
    left16 = left
    causal = rows >= cols
    strict = rows > cols
    eye = jnp.where(rows == cols, 1.0, 0.0).astype(F32)
    left_t = lax.broadcasted_iota(jnp.int32, (HD, HD), 1) < BLOCK

    log_gate = jnp.log1p(-1e-06 * gc_ref[...].astype(F32))
    tri = jnp.where(causal, 1.0, 0.0).astype(F32)[:, :BLOCK]
    cum = jnp.dot(tri, log_gate, precision=lax.Precision.HIGHEST, preferred_element_type=F32)
    gamma = jnp.exp(cum)
    beta = bc_ref[...].astype(F32) / 1000.0
    beta_g = beta * jnp.exp(-cum)
    last = gamma[BLOCK - 1 :]

    for j in range(kh):
        def conved(ref, taps, off, width):
            x = ref[...].astype(F32)
            ext = cat([carry[:, off : off + width], x], 0)
            out = conv(ext, taps)
            return out, x[BLOCK - 8 :]
        sl = slice(j * HD, (j + 1) * HD)
        qx, qtail = conved(q_ref.at[:, sl], cq_ref[:, sl], j * HD, HD)
        kx, ktail = conved(k_ref.at[:, sl], ck_ref[:, sl], kw + j * HD, HD)
        vs = slice(2 * j * HD, 2 * (j + 1) * HD)
        vx, vtail = conved(v_ref.at[:, vs], cv_ref[:, vs], 2 * kw + 2 * j * HD, 2 * HD)
        carry[:, j * HD : (j + 1) * HD] = qtail
        carry[:, kw + j * HD : kw + (j + 1) * HD] = ktail
        carry[:, 2 * kw + 2 * j * HD : 2 * kw + 2 * (j + 1) * HD] = vtail
        q = unit(qx) * HD ** (-0.5)
        k = unit(kx)
        kq = cat([k, q], 0)
        kq_hi, kq_lo = split(kq)
        kt = jnp.transpose(cat([k, k], 0))
        kt_hi, kt_lo = split(kt)
        kt_row = cat([kt_hi, kt_lo], 1)
        dots = fold(mxu(cat([kq_hi, kq_lo], 1), cat([kt_row, kt_row], 0)))
        b0 = jnp.broadcast_to(beta[:, 2 * j : 2 * j + 1], (BLOCK, HD))
        b1 = jnp.broadcast_to(beta[:, 2 * j + 1 : 2 * j + 2], (BLOCK, HD))
        low = jnp.where(strict, jnp.where(left, b0, b1) * dots[:BLOCK], 0.0)
        mix = jnp.where(causal, dots[BLOCK:], 0.0)
        inv = pair_inverse(low, eye, left16)
        ih, il = split(inv)
        rh, rl = split(pltpu.roll(inv, BLOCK, 1))
        t0 = jnp.where(left16, ih, rl)
        t1 = jnp.where(left16, rh, il)
        mh, ml = split(mix)
        m2 = jnp.where(left16, mh, ml)
        k2 = jnp.where(left_t, kt_hi, kt_lo)
        km = cat([k2, m2], 0)
        km4 = cat([km, km], 1)
        kq3 = cat([kq_hi, kq_lo, kq_hi], 1)
        for a, (t, b) in enumerate(((t0, b0), (t1, b1))):
            h = 2 * j + a
            s = state[h]
            s_hi, s_lo = split(s)
            z = mxu(kq3, cat([s_hi, s_hi, s_lo], 0))
            bg = beta_g[:, h : h + 1]
            right = cat([bg * vx[:, a * HD : (a + 1) * HD] - b * z[:BLOCK, :HD], -b * z[:BLOCK, HD:]], 1)
            r_hi, r_lo = split(right)
            u = mxu(cat([t, t], 1), cat([r_hi, r_hi, r_lo, r_lo], 0))
            u_hi, u_lo = split(u)
            ds = mxu(km4, cat([u_hi, u_hi, u_lo, u_lo], 0))
            g = gamma[:, h : h + 1]
            o = g * (z[BLOCK:] + ds[HD:])
            state[h] = last[:, h : h + 1] * (s + ds[:HD])
            base_ref[:, h * HD : (h + 1) * HD] = o[:, :HD]
            o_hi, o_lo = split(o[:, HD:])
            map_ref[:, 2 * h * HD : (2 * h + 1) * HD] = o_hi
            map_ref[:, (2 * h + 1) * HD : (2 * h + 2) * HD] = o_lo

    @pl.when(n == pl.num_programs(0) - 1)
    def _():
        fin_ref[...] = state[...]


def run_scan(q, k, v, gc, bc, halo, cq, ck, cv):
    rows = q.shape[0]
    kw, vw = q.shape[1], v.shape[1]
    vh = vw // HD
    row_spec = lambda w: pl.BlockSpec((BLOCK, w), lambda n: (n, 0))
    full = lambda a: pl.BlockSpec(a.shape, lambda n: (0,) * a.ndim)
    return pl.pallas_call(
        scan_kernel,
        grid=(rows // BLOCK,),
        in_specs=[row_spec(kw), row_spec(kw), row_spec(vw), row_spec(vh), row_spec(vh),
                  full(halo), full(cq), full(ck), full(cv)],
        out_specs=[row_spec(vw), row_spec(2 * vw), pl.BlockSpec((vh, HD, 2 * HD), lambda n: (0, 0, 0))],
        out_shape=[jax.ShapeDtypeStruct((rows, vw), F32),
                   jax.ShapeDtypeStruct((rows, 2 * vw), BF16),
                   jax.ShapeDtypeStruct((vh, HD, 2 * HD), F32)],
        scratch_shapes=[pltpu.VMEM((vh, HD, 2 * HD), F32), pltpu.VMEM((8, 2 * kw + vw), F32)],
        compiler_params=pltpu.CompilerParams(dimension_semantics=("arbitrary",), vmem_limit_bytes=56 << 20),
        name="scan",
    )(q, k, v, gc, bc, halo, cq.astype(F32), ck.astype(F32), cv.astype(F32))


def dot3(a, b):
    a_hi, a_lo = split(a)
    b_hi, b_lo = split(b)
    return mxu(cat([a_hi, a_lo, a_hi], 1), cat([b_hi, b_hi, b_lo], 0))


def then(later, earlier):
    out = dot3(later[:, HD:], earlier)
    return cat([later[:, :HD] + out[:, :HD], out[:, HD:]], 1)


def vmem_call(body, outs, scratch, name, scalars, *arrays):
    return pl.pallas_call(
        body,
        in_specs=[pl.BlockSpec(memory_space=pltpu.SMEM)] + [pl.BlockSpec(memory_space=pltpu.VMEM)] * len(arrays),
        out_specs=[pl.BlockSpec(memory_space=pltpu.VMEM)] * len(outs),
        out_shape=[jax.ShapeDtypeStruct(s, F32) for s in outs],
        scratch_shapes=[pltpu.VMEM(s, F32) for s in scratch],
        name=name,
    )(scalars, *arrays)


def pair_kernel(pos, kept, got, early_ref, both_ref):
    first = pos[2] == 0
    for h in range(kept.shape[0]):
        mine, other = kept[h], got[h]
        early = jnp.where(first, mine, other)
        late = jnp.where(first, other, mine)
        early_ref[h] = early
        both_ref[h] = then(late, early)


def prefix_kernel(pos, a0, a1, a2, a3, pre_ref, tot_ref, line):
    z = pos[1]
    for d, a in enumerate((a0, a1, a2, a3)):
        line[(z - d + Z_CHIPS) % Z_CHIPS] = a[...]
    r = lax.broadcasted_iota(jnp.int32, (HD, 2 * HD), 0)
    c = lax.broadcasted_iota(jnp.int32, (HD, 2 * HD), 1)
    pre_ref[0] = jnp.where(r + HD == c, 1.0, 0.0).astype(F32)
    run = line[0]
    for i in range(1, Z_CHIPS):
        pre_ref[i] = run
        run = then(line[i], run)
    tot_ref[...] = run


def entry_kernel(pos, a0, a1, a2, a3, pre, out_ref, line, states):
    x = pos[0]
    for d, a in enumerate((a0, a1, a2, a3)):
        line[(x - d + X_CHIPS) % X_CHIPS] = a[...]
    run = jnp.zeros((HD, HD), F32)
    for i in range(X_CHIPS):
        states[i] = run
        if i + 1 < X_CHIPS:
            run = line[i, :, :HD] + dot3(line[i, :, HD:], run)
    mine = states[x]
    out_ref[0] = mine
    for i in range(1, Z_CHIPS):
        out_ref[i] = pre[i, :, :HD] + dot3(pre[i, :, HD:], mine)


def cores_kernel(pos, a0, a1, a2, a3, early, keep_ref, send_ref, line):
    z, first = pos[1], pos[2] == 0
    for d, a in enumerate((a0, a1, a2, a3)):
        line[(z - d + Z_CHIPS) % Z_CHIPS] = a[...]
    for h in range(Z_CHIPS):
        s = line[h]
        t = early[h, :, :HD] + dot3(early[h, :, HD:], s)
        keep_ref[h] = jnp.where(first, s, t)
        send_ref[h] = jnp.where(first, t, s)


def out_kernel(pos, base_ref, map_ref, kept, got, gate_ref, gain_ref, y_ref):
    h = pl.program_id(0)
    per = kept.shape[0]
    own = (h // per) == pos[2]
    s = jnp.where(own, kept[h % per], got[h % per])
    row = wide(s)
    o = base_ref[...] + fold(mxu(map_ref[...], cat([row, row], 0)))
    g = gate_ref[...].astype(F32)
    y = o * lax.rsqrt(jnp.mean(o * o, -1, keepdims=True) + 1e-06) * gain_ref[...] * silu(g)
    y_ref[...] = y.astype(BF16)


def run_out(pos, base, maps, kept, got, gate, gain):
    rows, width = base.shape
    col = lambda w: pl.BlockSpec((rows, w), lambda h: (0, h))
    full = lambda a: pl.BlockSpec(a.shape, lambda h: (0,) * a.ndim)
    return pl.pallas_call(
        out_kernel,
        grid=(width // HD,),
        in_specs=[pl.BlockSpec(memory_space=pltpu.SMEM), col(HD), col(2 * HD), full(kept), full(got), col(HD), full(gain)],
        out_specs=col(HD),
        out_shape=jax.ShapeDtypeStruct((rows, width), BF16),
        name="out",
    )(pos, base, maps, kept, got, gate, gain)


def ctx_route(dx, dz, dc):
    def dest(i):
        x, z, c = i // (Z_CHIPS * CORES), (i // CORES) % Z_CHIPS, i % CORES
        return ((x + dx) % X_CHIPS * Z_CHIPS + (z + dz) % Z_CHIPS) * CORES + (c + dc) % CORES
    return [(i, dest(i)) for i in range(X_CHIPS * Z_CHIPS * CORES)]


def row_of(array, index):
    return lax.dynamic_index_in_dim(array, index, 0, keepdims=False)


def shards(query_raw, key_raw, value_raw, gate_branch, gate_code, beta_code,
           conv_query, conv_key, conv_value, norm_gain, out_weight):
    tok_rows = query_raw.shape[0]
    vh = value_raw.shape[1] // HD
    half = vh // CORES
    ctx = lax.axis_index("ctx")
    head = lax.axis_index("head")
    heads = lax.axis_size("head")
    x, z, core = ctx // (Z_CHIPS * CORES), (ctx // CORES) % Z_CHIPS, ctx % CORES
    pos = jnp.stack([x, z, core]).astype(jnp.int32)
    send = lambda a, dx, dz, dc: lax.ppermute(a, "ctx", ctx_route(dx, dz, dc))
    turn = lambda a, d: lax.ppermute(a, "head", [(i, (i + d) % heads) for i in range(heads)])

    rim = cat([a[tok_rows - 8 :] for a in (query_raw, key_raw, value_raw)], 1)
    n_ctx = lax.axis_size("ctx")
    halo = lax.ppermute(rim, "ctx", [(i, i + 1) for i in range(n_ctx - 1)])

    w_rows = out_weight.shape[0] // CORES
    w_mine = lax.dynamic_slice_in_dim(out_weight, core * w_rows, w_rows, 0)
    w_got = [turn(w_mine, d) for d in range(1, heads)]

    base, maps, fin = run_scan(query_raw, key_raw, value_raw, gate_code, beta_code, halo,
                               conv_query, conv_key, conv_value)

    kept = lax.dynamic_slice_in_dim(fin, core * half, half, 0)
    away = lax.dynamic_slice_in_dim(fin, (1 - core) * half, half, 0)
    early, both = vmem_call(pair_kernel, [kept.shape] * 2, [], "pair", pos, kept, send(away, 0, 0, 1))
    lines = [row_of(both, z)] + [send(row_of(both, (z + d) % Z_CHIPS), 0, d, 0) for d in range(1, Z_CHIPS)]
    pre, tot = vmem_call(prefix_kernel, [(Z_CHIPS, HD, 2 * HD), (HD, 2 * HD)], [(Z_CHIPS, HD, 2 * HD)],
                         "prefix", pos, *lines)
    tots = [tot] + [send(tot, d, 0, 0) for d in range(1, X_CHIPS)]
    entry, = vmem_call(entry_kernel, [(Z_CHIPS, HD, HD)], [(X_CHIPS, HD, 2 * HD), (X_CHIPS, HD, HD)],
                       "entry", pos, *tots, pre)
    backs = [row_of(entry, z)] + [send(row_of(entry, (z + d) % Z_CHIPS), 0, d, 0) for d in range(1, Z_CHIPS)]
    own, lent = vmem_call(cores_kernel, [(half, HD, HD)] * 2, [(Z_CHIPS, HD, HD)], "cores", pos, *backs, early)
    got = send(lent, 0, 0, 1)

    w_other = [send(w, 0, 0, 1) for w in w_got]

    y = run_out(pos, base, maps, own, got, gate_branch, norm_gain.reshape(1, HD))
    rows = tok_rows // heads
    piece = lambda i: lax.dynamic_slice_in_dim(y, i * rows, rows, 0)
    y_got = [turn(piece((head + d) % heads), d) for d in range(1, heads)]
    total = jnp.dot(piece(head), out_weight, preferred_element_type=F32)
    for yd, wm, wo in zip(y_got, w_got, w_other):
        w = jnp.where(core == 0, cat([wm, wo], 0), cat([wo, wm], 0))
        total = total + jnp.dot(yd, w, preferred_element_type=F32)
    return total.astype(BF16)


def solution(mesh):
    return jax.shard_map(
        shards,
        mesh=mesh,
        in_specs=(P("ctx", "head"),) * 6 + (P(None, "head"),) * 3 + (P(), P("head", None)),
        out_specs=P(("ctx", "head"), None),
        check_vma=False,
    )
```

time: 845 us -> 229 us (0.27)
  waiting for transfers between devices: 308 us -> 27.8 us
  matrix products: 283 us -> 18.6 us
  starting transfers between devices: 170 us -> 36.6 us
  Pallas kernels: 0 us -> 127 us
  other arithmetic: 36.6 us -> 2.47 us
  between operations: 14.1 us -> 0.2 us
    dot_general x114 -> x4, matrix products: 283 us -> 18.6 us  [the longest x3 15 us: shards(): total = total + jnp.dot(yd, w, preferred_element_type=F32)]
    ppermute x34 -> x21, waiting for transfers between devices: 189 us -> 27.8 us  [the longest x14 15 us: shards(): send = lambda a, dx, dz, dc: lax.ppermute(a, 'ctx', ctx_route(dx, dz, dc))]
    ppermute x34 -> x21, starting transfers between devices: 170 us -> 36.6 us  [the longest x14 23.6 us: shards(): send = lambda a, dx, dz, dc: lax.ppermute(a, 'ctx', ctx_route(dx, dz, dc))]
    pallas_call x0 -> x6, Pallas kernels: none -> 127 us  [the longest x1 107 us: run_scan(): pl.pallas_call(scan_kernel, grid=(rows // BLOCK,), in_specs=[row_spec(kw)...]
    reduce_scatter x1 -> x0, waiting for transfers between devices: 119 us -> none  [shards(): lax.psum_scatter(jnp.dot(normed, out_weight, preferred_element_type=jnp.f...]
    mul x7 -> x0, other arithmetic: 11.6 us -> none  [the longest x2 5.14 us: causal_conv(): return jax.nn.silu(running)]
  transfers between devices with their start and end apart: 35 -> 21, of which waited for: 32 -> 11; matrix products, arithmetic and copies ran while one was open for 16% -> 11% of each run, Pallas kernels for 0% -> 56%
where the time goes in v1:
time: 229 us; the launch traced here: 227 us
  Pallas kernels  127 us (55%)
  starting transfers between devices  36.6 us (16%)
  waiting for transfers between devices  27.8 us (12%)
  matrix products  18.6 us (8%)
  local copies, waits for them, and re-layouts  14.9 us (7%)
  other arithmetic  2.47 us (1%)
    pallas_call x1, Pallas kernels, run_scan(): pl.pallas_call(scan_kernel, grid=(rows // BLOCK,), in_specs=[row_spec(kw)...  107 us
    ppermute x14, starting transfers between devices, shards(): send = lambda a, dx, dz, dc: lax.ppermute(a, 'ctx', ctx_route(dx, dz, dc))  23.6 us
    ppermute x14, waiting for transfers between devices, shards(): send = lambda a, dx, dz, dc: lax.ppermute(a, 'ctx', ctx_route(dx, dz, dc))  15 us
    dot_general x3, matrix products, shards(): total = total + jnp.dot(yd, w, preferred_element_type=F32)  15 us
    ppermute x6, waiting for transfers between devices, shards(): lax.ppermute(a, 'head', [(i, (i + d) % heads) for i in range(heads)])  12.8 us
    pallas_call x4, Pallas kernels, vmem_call(): pl.pallas_call(body, in_specs=[pl.BlockSpec(memory_space=pltpu.SMEM)] + [...  9.93 us
    pallas_call x1, Pallas kernels, run_out(): pl.pallas_call(out_kernel, grid=(width // HD,), in_specs=[pl.BlockSpec(me...  9.39 us
    ppermute x6, starting transfers between devices, shards(): lax.ppermute(a, 'head', [(i, (i + d) % heads) for i in range(heads)])  8.04 us
  transfers between devices with their start and end apart: 21, of which 11 were waited for; matrix products, arithmetic and copies ran while one was open for 11% of the time, Pallas kernels for 56%

profile of v1, /device:TPU:1, one launch (start us, length us, event | category | flops | bytes accessed | tf_op | source)
XLA Modules:
  0.0 227.1 jit_solution(17328028720771641141)
XLA Ops:
  2.0 2.2 collective-permute-start.13
  7.2 4.9 %collective-permute-start = (bf16[8,2048]{1,0:T(8,128)(2,1)S(1)}, bf16[8,2048]{1,0:T(8,128)(2,1)S(1)}, u32[]{:S(2)}, u32[]{:S(2)}) collective-permute-start(bf16[8,2048]{1,0:T(8,128)(2,1)S(1)} %pad_maximum_fusion), channel_id=1, source_target_pairs={{0,4},{4,8},{8,12},{12,16},{16,20},{20,24},{24,28},{28,32},{32,36}... | collective-permute-start | bytes 98312 | tf_op jit(solution)/shard_map/ppermute | solution.py:315
  16.7 107.3 %scan.1 = (f32[1024,1024]{1,0:T(8,128)}, bf16[1024,2048]{1,0:T(8,128)(2,1)}, f32[8,128,256]{2,1,0:T(8,128)}) custom-call(bf16[1024,512]{1,0:T(8,128)(2,1)} %q_ref.1, bf16[1024,512]{1,0:T(8,128)(2,1)} %k_ref.1, bf16[1024,1024]{1,0:T(8,128)(2,1)} %v_ref.1, s32[1024,8]{1,0:T(8,128)} %copy.12.gc_ref, s32[1024,8]{1,0:T(8,128)} %copy.13.bc_ref, ...), custom_call_target="tpu_custom_call" | custom-call | tf_op jit(solution)/shard_map/scan/pallas_call | solution.py:176
  124.0 2.1 constant_dynamic-slice_fusion.4
  128.8 2.4 %pair.1 = (f32[4,128,256]{2,1,0:T(8,128)}, f32[4,128,256]{2,1,0:T(8,128)}) custom-call(s32[3]{0:T(128)} %pad_add_fusion.pos, f32[4,128,256]{2,1,0:T(8,128)} %get-tuple-element.27.kept, f32[4,128,256]{2,1,0:T(8,128)} %copy-done), custom_call_target="tpu_custom_call" | custom-call | tf_op jit(solution)/shard_map/pair/pallas_call | solution.py:203
  136.3 2.8 %collective-permute-done.2.a1 = f32[128,256]{1,0:T(8,128)S(1)} collective-permute-done((f32[128,256]{1,0:T(8,128)S(1)}, f32[128,256]{1,0:T(8,128)S(1)}, u32[]{:S(2)}, u32[]{:S(2)}) %collective-permute-start.2) | collective-permute-done | bytes 131104 | tf_op jit(solution)/shard_map/ppermute | solution.py:310
  140.1 2.5 %collective-permute-done.3.a2 = f32[128,256]{1,0:T(8,128)S(1)} collective-permute-done((f32[128,256]{1,0:T(8,128)S(1)}, f32[128,256]{1,0:T(8,128)S(1)}, u32[]{:S(2)}, u32[]{:S(2)}) %collective-permute-start.3) | collective-permute-done | bytes 131104 | tf_op jit(solution)/shard_map/ppermute | solution.py:310
  143.8 2.5 %prefix.1 = (f32[4,128,256]{2,1,0:T(8,128)}, f32[128,256]{1,0:T(8,128)}) custom-call(s32[3]{0:T(128)} %pad_add_fusion.pos, f32[128,256]{1,0:T(8,128)} %get-tuple-element.31.a0, f32[128,256]{1,0:T(8,128)} %copy-done.3, f32[128,256]{1,0:T(8,128)} %copy-done.4, f32[128,256]{1,0:T(8,128)} %copy-done.6), custom_call_target="tpu_custom_call" | custom-call | tf_op jit(solution)/shard_map/prefix/pallas_call | solution.py:203
  147.5 2.2 collective-permute-start.20
  149.7 2.4 %collective-permute-start.6 = (f32[128,256]{1,0:T(8,128)}, f32[128,256]{1,0:T(8,128)S(1)}, u32[]{:S(2)}, u32[]{:S(2)}) collective-permute-start(f32[128,256]{1,0:T(8,128)} %get-tuple-element.18.a0), channel_id=1, source_target_pairs={{0,64},{4,68},{8,72},{12,76},{16,80},{20,84},{24,88},{28,92},{32,9... | collective-permute-start | bytes 393224 | tf_op jit(solution)/shard_map/ppermute | solution.py:310
  153.3 3.6 %collective-permute-done.6.a2 = f32[128,256]{1,0:T(8,128)S(1)} collective-permute-done((f32[128,256]{1,0:T(8,128)}, f32[128,256]{1,0:T(8,128)S(1)}, u32[]{:S(2)}, u32[]{:S(2)}) %collective-permute-start.6) | collective-permute-done | bytes 131104 | tf_op jit(solution)/shard_map/ppermute | solution.py:310
  158.1 2.8 %entry.1 = f32[4,128,128]{2,1,0:T(8,128)} custom-call(s32[3]{0:T(128)} %pad_add_fusion.pos, f32[128,256]{1,0:T(8,128)} %get-tuple-element.18.a0, f32[128,256]{1,0:T(8,128)} %copy-done.2, f32[128,256]{1,0:T(8,128)} %copy-done.5, f32[128,256]{1,0:T(8,128)} %copy-done.7, f32[4,128,256]{2,1,0:T(8,128)} %get-tuple-element.19.pre), custom_call_target="tpu_custom_call" | custom-call | tf_op jit(solution)/shard_map/entry/pallas_call | solution.py:203
  162.4 3.0 %collective-permute-start.10 = (f32[128,128]{1,0:T(8,128)S(1)}, f32[128,128]{1,0:T(8,128)S(1)}, u32[]{:S(2)}, u32[]{:S(2)}) collective-permute-start(f32[128,128]{1,0:T(8,128)S(1)} %get-tuple-element.32), channel_id=1, source_target_pairs={{0,24},{4,28},{8,0},{12,4},{16,8},{20,12},{24,16},{28,20},{32,56},... | collective-permute-start | bytes 196616 | tf_op jit(solution)/shard_map/ppermute | solution.py:310
  166.9 3.5 %collective-permute-start.9 = (f32[128,128]{1,0:T(8,128)S(1)}, f32[128,128]{1,0:T(8,128)S(1)}, u32[]{:S(2)}, u32[]{:S(2)}) collective-permute-start(f32[128,128]{1,0:T(8,128)S(1)} %get-tuple-element.33), channel_id=1, source_target_pairs={{0,16},{4,20},{8,24},{12,28},{16,0},{20,4},{24,8},{28,12},{32,48},... | collective-permute-start | bytes 196616 | tf_op jit(solution)/shard_map/ppermute | solution.py:310
  172.7 2.3 %cores.1 = (f32[4,128,128]{2,1,0:T(8,128)}, f32[4,128,128]{2,1,0:T(8,128)}) custom-call(s32[3]{0:T(128)} %pad_add_fusion.pos, f32[128,128]{1,0:T(8,128)} %get-tuple-element.35.a0, f32[128,128]{1,0:T(8,128)} %copy-done.9, f32[128,128]{1,0:T(8,128)} %copy-done.10, f32[128,128]{1,0:T(8,128)} %copy-done.8, f32[4,128,256]{2,1,0:T(8,128)} %get-tuple-element.20.early), custom_call_target="tpu_custom_call" | custom-call | tf_op jit(solution)/shard_map/cores/pallas_call | solution.py:203
  175.0 5.0 %collective-permute-start.11 = (f32[4,128,128]{2,1,0:T(8,128)}, f32[4,128,128]{2,1,0:T(8,128)S(1)}, u32[]{:S(2)}, u32[]{:S(2)}) collective-permute-start(f32[4,128,128]{2,1,0:T(8,128)} %get-tuple-element.22), channel_id=1, source_target_pairs={{0,4},{4,0},{8,12},{12,8},{16,20},{20,16},{24,28},{28,24},{32,36},... | collective-permute-start | bytes 786440 | tf_op jit(solution)/shard_map/ppermute | solution.py:310
  182.1 9.4 %out.1 = bf16[1024,1024]{1,0:T(8,128)(2,1)} custom-call(s32[3]{0:T(128)} %pad_add_fusion.pos, f32[1024,1024]{1,0:T(8,128)} %get-tuple-element.14.base_ref, bf16[1024,2048]{1,0:T(8,128)(2,1)} %get-tuple-element.15.map_ref, f32[4,128,128]{2,1,0:T(8,128)} %get-tuple-element.21.kept, f32[4,128,128]{2,1,0:T(8,128)} %copy-done.1, bf16[1024,1024]{1,0:T(8,128)(2,1)} %gate_ref.1, ...), custom_call_target="tpu_custom_call" | custom-call | tf_op jit(solution)/shard_map/out/pallas_call | solution.py:279
  193.4 2.3 %collective-permute-start.18 = (bf16[256,1024]{1,0:T(8,128)(2,1)S(1)}, bf16[256,1024]{1,0:T(8,128)(2,1)S(1)}, u32[]{:S(2)}, u32[]{:S(2)}) collective-permute-start(bf16[256,1024]{1,0:T(8,128)(2,1)S(1)} %get-tuple-element.24), channel_id=1, source_target_pairs={{0,3},{1,0},{2,1},{3,2},{4,7},{5,4},{6,5},{7,6},{8,11},{9,8},{10,9... | collective-permute-start | bytes 1572872 | tf_op jit(solution)/shard_map/ppermute | solution.py:311
  195.7 3.6 %fusion.25 = f32[256,2048]{1,0:T(8,128)S(1)} fusion(bf16[1024,2048]{1,0:T(8,128)(2,1)} %param.21, bf16[1024,1024]{1,0:T(8,128)(2,1)} %out.1, s32[]{:T(128)S(6)} %select_n.116), kind=kOutput, calls=%fused_computation.28 | convolution fusion | flops 1073741824 | bytes 6815748 | tf_op jit(solution)/shard_map/dot_general | solution.py:343
  199.3 8.0 %collective-permute-done.12 = bf16[256,1024]{1,0:T(8,128)(2,1)S(1)} collective-permute-done((bf16[256,1024]{1,0:T(8,128)(2,1)S(1)}, bf16[256,1024]{1,0:T(8,128)(2,1)S(1)}, u32[]{:S(2)}, u32[]{:S(2)}) %collective-permute-start.12) | collective-permute-done | bytes 524320 | tf_op jit(solution)/shard_map/ppermute | solution.py:311
  207.4 4.2 %fusion.22 = f32[256,2048]{1,0:T(8,128)S(1)} fusion(f32[256,2048]{1,0:T(8,128)S(1)} %fusion.25, bf16[256,1024]{1,0:T(8,128)(2,1)S(1)} %collective-permute-done.12, bf16[512,2048]{1,0:T(8,128)(2,1)} %collective-permute-done.14, bf16[512,2048]{1,0:T(8,128)(2,1)} %collective-permute-done.13, pred[]{:T(512)S(6)} %eq.17), kind=kOutput, calls=%fused_computation.25 | convolution fusion | flops 1093140480 | bytes 8912897 | tf_op jit(solution)/shard_map/dot_general | solution.py:346
  211.6 4.7 %fusion.12 = f32[256,2048]{1,0:T(8,128)S(1)} fusion(bf16[256,1024]{1,0:T(8,128)(2,1)S(1)} %collective-permute-done.18, bf16[512,2048]{1,0:T(8,128)(2,1)} %collective-permute-done.20, bf16[512,2048]{1,0:T(8,128)(2,1)} %collective-permute-done.19, pred[]{:T(512)S(6)} %eq.17), kind=kOutput, calls=%fused_computation.15 | convolution fusion | flops 1092616192 | bytes 6815745 | tf_op jit(solution)/shard_map/dot_general | solution.py:346
  216.4 4.7 %collective-permute-done.15 = bf16[256,1024]{1,0:T(8,128)(2,1)S(1)} collective-permute-done((bf16[256,1024]{1,0:T(8,128)(2,1)S(1)}, bf16[256,1024]{1,0:T(8,128)(2,1)S(1)}, u32[]{:S(2)}, u32[]{:S(2)}) %collective-permute-start.15) | collective-permute-done | bytes 524320 | tf_op jit(solution)/shard_map/ppermute | solution.py:311
  221.1 6.0 %fusion.24 = bf16[256,2048]{1,0:T(8,128)(2,1)} fusion(f32[256,2048]{1,0:T(8,128)S(1)} %fusion.12, f32[256,2048]{1,0:T(8,128)S(1)} %fusion.22, bf16[256,1024]{1,0:T(8,128)(2,1)S(1)} %collective-permute-done.15, bf16[512,2048]{1,0:T(8,128)(2,1)} %collective-permute-done.17, bf16[512,2048]{1,0:T(8,128)(2,1)} %collective-permute-done.16, pred[]{:T(512)S(6)} %eq.17), kind=kOutput, calls=%fused_computation.27 | convolution fusion | flops 1094189056 | bytes 9961473 | tf_op jit(solution)/shard_map/dot_general | solution.py:346
  (80 shorter events, 32.2 us)
Async XLA Ops:
  0.0 14.2 %copy-start.14 = (bf16[4,1024]{1,0:T(4,128)(2,1)S(1)}, bf16[4,1024]{1,0:T(4,128)(2,1)}, u32[]{:S(2)}) copy-start(bf16[4,1024]{1,0:T(4,128)(2,1)} %param.19) | copy-start | bytes 24580
  0.0 14.8 %copy-start.15 = (bf16[4,512]{1,0:T(4,128)(2,1)S(1)}, bf16[4,512]{1,0:T(4,128)(2,1)}, u32[]{:S(2)}) copy-start(bf16[4,512]{1,0:T(4,128)(2,1)} %param.17) | copy-start | bytes 12292
  0.0 15.4 %copy-start.16 = (bf16[4,512]{1,0:T(4,128)(2,1)S(1)}, bf16[4,512]{1,0:T(4,128)(2,1)}, u32[]{:S(2)}) copy-start(bf16[4,512]{1,0:T(4,128)(2,1)} %param.18) | copy-start | bytes 12292
  2.0 124.1 %collective-permute-start.13 = (bf16[512,2048]{1,0:T(8,128)(2,1)S(1)}, bf16[512,2048]{1,0:T(8,128)(2,1)}, u32[]{:S(2)}, u32[]{:S(2)}) collective-permute-start(bf16[512,2048]{1,0:T(8,128)(2,1)S(1)} %constant_dynamic-slice_fusion.2), channel_id=1, source_target_pairs={{0,1},{1,2},{2,3},{3,0},{4,5},{5,6},{6,7},{7,4},{8,9},{9,10},{10,1... | collective-permute-start | bytes 6291464 | tf_op jit(solution)/shard_map/ppermute | solution.py:311
  4.1 143.3 %collective-permute-start.19 = (bf16[512,2048]{1,0:T(8,128)(2,1)S(1)}, bf16[512,2048]{1,0:T(8,128)(2,1)}, u32[]{:S(2)}, u32[]{:S(2)}) collective-permute-start(bf16[512,2048]{1,0:T(8,128)(2,1)S(1)} %constant_dynamic-slice_fusion.2), channel_id=1, source_target_pairs={{0,3},{1,0},{2,1},{3,2},{4,7},{5,4},{6,5},{7,6},{8,11},{9,8},{10,9... | collective-permute-start | bytes 6291464 | tf_op jit(solution)/shard_map/ppermute | solution.py:311
  5.7 174.3 %collective-permute-start.16 = (bf16[512,2048]{1,0:T(8,128)(2,1)S(1)}, bf16[512,2048]{1,0:T(8,128)(2,1)}, u32[]{:S(2)}, u32[]{:S(2)}) collective-permute-start(bf16[512,2048]{1,0:T(8,128)(2,1)S(1)} %constant_dynamic-slice_fusion.2), channel_id=1, source_target_pairs={{0,2},{1,3},{2,0},{3,1},{4,6},{5,7},{6,4},{7,5},{8,10},{9,11},{10,... | collective-permute-start | bytes 6291464 | tf_op jit(solution)/shard_map/ppermute | solution.py:311
  7.2 8.8 %collective-permute-start = (bf16[8,2048]{1,0:T(8,128)(2,1)S(1)}, bf16[8,2048]{1,0:T(8,128)(2,1)S(1)}, u32[]{:S(2)}, u32[]{:S(2)}) collective-permute-start(bf16[8,2048]{1,0:T(8,128)(2,1)S(1)} %pad_maximum_fusion), channel_id=1, source_target_pairs={{0,4},{4,8},{8,12},{12,16},{16,20},{20,24},{24,28},{28,32},{32,36}... | collective-permute-start | bytes 98312 | tf_op jit(solution)/shard_map/ppermute | solution.py:315
  126.1 1.9 collective-permute-start.1
  126.1 81.3 %collective-permute-start.14 = (bf16[512,2048]{1,0:T(8,128)(2,1)}, bf16[512,2048]{1,0:T(8,128)(2,1)}, u32[]{:S(2)}, u32[]{:S(2)}) collective-permute-start(bf16[512,2048]{1,0:T(8,128)(2,1)} %collective-permute-done.13), channel_id=1, source_target_pairs={{0,4},{4,0},{8,12},{12,8},{16,20},{20,16},{24,28},{28,24},{32,36},... | collective-permute-start | bytes 6291464 | tf_op jit(solution)/shard_map/ppermute | solution.py:310
  133.0 6.1 %collective-permute-start.2 = (f32[128,256]{1,0:T(8,128)S(1)}, f32[128,256]{1,0:T(8,128)S(1)}, u32[]{:S(2)}, u32[]{:S(2)}) collective-permute-start(f32[128,256]{1,0:T(8,128)S(1)} %get-tuple-element.30), channel_id=1, source_target_pairs={{0,8},{4,12},{8,16},{12,20},{16,24},{20,28},{24,0},{28,4},{32,40},... | collective-permute-start | bytes 393224 | tf_op jit(solution)/shard_map/ppermute | solution.py:310
  134.6 7.9 %collective-permute-start.3 = (f32[128,256]{1,0:T(8,128)S(1)}, f32[128,256]{1,0:T(8,128)S(1)}, u32[]{:S(2)}, u32[]{:S(2)}) collective-permute-start(f32[128,256]{1,0:T(8,128)S(1)} %get-tuple-element.29), channel_id=1, source_target_pairs={{0,16},{4,20},{8,24},{12,28},{16,0},{20,4},{24,8},{28,12},{32,48},... | collective-permute-start | bytes 393224 | tf_op jit(solution)/shard_map/ppermute | solution.py:310
  139.1 4.0 %collective-permute-start.4 = (f32[128,256]{1,0:T(8,128)S(1)}, f32[128,256]{1,0:T(8,128)S(1)}, u32[]{:S(2)}, u32[]{:S(2)}) collective-permute-start(f32[128,256]{1,0:T(8,128)S(1)} %get-tuple-element.28), channel_id=1, source_target_pairs={{0,24},{4,28},{8,0},{12,4},{16,8},{20,12},{24,16},{28,20},{32,56},... | collective-permute-start | bytes 393224 | tf_op jit(solution)/shard_map/ppermute | solution.py:310
  146.3 5.9 %collective-permute-start.5 = (f32[128,256]{1,0:T(8,128)}, f32[128,256]{1,0:T(8,128)S(1)}, u32[]{:S(2)}, u32[]{:S(2)}) collective-permute-start(f32[128,256]{1,0:T(8,128)} %get-tuple-element.18.a0), channel_id=1, source_target_pairs={{0,32},{4,36},{8,40},{12,44},{16,48},{20,52},{24,56},{28,60},{32,6... | collective-permute-start | bytes 393224 | tf_op jit(solution)/shard_map/ppermute | solution.py:310
  147.5 64.2 %collective-permute-start.20 = (bf16[512,2048]{1,0:T(8,128)(2,1)}, bf16[512,2048]{1,0:T(8,128)(2,1)}, u32[]{:S(2)}, u32[]{:S(2)}) collective-permute-start(bf16[512,2048]{1,0:T(8,128)(2,1)} %collective-permute-done.19), channel_id=1, source_target_pairs={{0,4},{4,0},{8,12},{12,8},{16,20},{20,16},{24,28},{28,24},{32,36},... | collective-permute-start | bytes 6291464 | tf_op jit(solution)/shard_map/ppermute | solution.py:310
  149.7 7.2 %collective-permute-start.6 = (f32[128,256]{1,0:T(8,128)}, f32[128,256]{1,0:T(8,128)S(1)}, u32[]{:S(2)}, u32[]{:S(2)}) collective-permute-start(f32[128,256]{1,0:T(8,128)} %get-tuple-element.18.a0), channel_id=1, source_target_pairs={{0,64},{4,68},{8,72},{12,76},{16,80},{20,84},{24,88},{28,92},{32,9... | collective-permute-start | bytes 393224 | tf_op jit(solution)/shard_map/ppermute | solution.py:310
  152.1 5.3 %collective-permute-start.7 = (f32[128,256]{1,0:T(8,128)}, f32[128,256]{1,0:T(8,128)S(1)}, u32[]{:S(2)}, u32[]{:S(2)}) collective-permute-start(f32[128,256]{1,0:T(8,128)} %get-tuple-element.18.a0), channel_id=1, source_target_pairs={{0,96},{4,100},{8,104},{12,108},{16,112},{20,116},{24,120},{28,124... | collective-permute-start | bytes 393224 | tf_op jit(solution)/shard_map/ppermute | solution.py:310
  162.4 4.5 %collective-permute-start.10 = (f32[128,128]{1,0:T(8,128)S(1)}, f32[128,128]{1,0:T(8,128)S(1)}, u32[]{:S(2)}, u32[]{:S(2)}) collective-permute-start(f32[128,128]{1,0:T(8,128)S(1)} %get-tuple-element.32), channel_id=1, source_target_pairs={{0,24},{4,28},{8,0},{12,4},{16,8},{20,12},{24,16},{28,20},{32,56},... | collective-permute-start | bytes 196616 | tf_op jit(solution)/shard_map/ppermute | solution.py:310
  165.4 5.0 %collective-permute-start.8 = (f32[128,128]{1,0:T(8,128)S(1)}, f32[128,128]{1,0:T(8,128)S(1)}, u32[]{:S(2)}, u32[]{:S(2)}) collective-permute-start(f32[128,128]{1,0:T(8,128)S(1)} %get-tuple-element.34), channel_id=1, source_target_pairs={{0,8},{4,12},{8,16},{12,20},{16,24},{20,28},{24,0},{28,4},{32,40},... | collective-permute-start | bytes 196616 | tf_op jit(solution)/shard_map/ppermute | solution.py:310
  166.9 5.2 %collective-permute-start.9 = (f32[128,128]{1,0:T(8,128)S(1)}, f32[128,128]{1,0:T(8,128)S(1)}, u32[]{:S(2)}, u32[]{:S(2)}) collective-permute-start(f32[128,128]{1,0:T(8,128)S(1)} %get-tuple-element.33), channel_id=1, source_target_pairs={{0,16},{4,20},{8,24},{12,28},{16,0},{20,4},{24,8},{28,12},{32,48},... | collective-permute-start | bytes 196616 | tf_op jit(solution)/shard_map/ppermute | solution.py:310
  175.0 6.4 %collective-permute-start.11 = (f32[4,128,128]{2,1,0:T(8,128)}, f32[4,128,128]{2,1,0:T(8,128)S(1)}, u32[]{:S(2)}, u32[]{:S(2)}) collective-permute-start(f32[4,128,128]{2,1,0:T(8,128)} %get-tuple-element.22), channel_id=1, source_target_pairs={{0,4},{4,0},{8,12},{12,8},{16,20},{20,16},{24,28},{28,24},{32,36},... | collective-permute-start | bytes 786440 | tf_op jit(solution)/shard_map/ppermute | solution.py:310
  180.0 41.1 %collective-permute-start.17 = (bf16[512,2048]{1,0:T(8,128)(2,1)}, bf16[512,2048]{1,0:T(8,128)(2,1)}, u32[]{:S(2)}, u32[]{:S(2)}) collective-permute-start(bf16[512,2048]{1,0:T(8,128)(2,1)} %collective-permute-done.16), channel_id=1, source_target_pairs={{0,4},{4,0},{8,12},{12,8},{16,20},{20,16},{24,28},{28,24},{32,36},... | collective-permute-start | bytes 6291464 | tf_op jit(solution)/shard_map/ppermute | solution.py:310
  192.9 14.4 %collective-permute-start.12 = (bf16[256,1024]{1,0:T(8,128)(2,1)S(1)}, bf16[256,1024]{1,0:T(8,128)(2,1)S(1)}, u32[]{:S(2)}, u32[]{:S(2)}) collective-permute-start(bf16[256,1024]{1,0:T(8,128)(2,1)S(1)} %get-tuple-element.25), channel_id=1, source_target_pairs={{0,1},{1,2},{2,3},{3,0},{4,5},{5,6},{6,7},{7,4},{8,9},{9,10},{10,1... | collective-permute-start | bytes 1572872 | tf_op jit(solution)/shard_map/ppermute | solution.py:311
  193.4 18.2 %collective-permute-start.18 = (bf16[256,1024]{1,0:T(8,128)(2,1)S(1)}, bf16[256,1024]{1,0:T(8,128)(2,1)S(1)}, u32[]{:S(2)}, u32[]{:S(2)}) collective-permute-start(bf16[256,1024]{1,0:T(8,128)(2,1)S(1)} %get-tuple-element.24), channel_id=1, source_target_pairs={{0,3},{1,0},{2,1},{3,2},{4,7},{5,4},{6,5},{7,6},{8,11},{9,8},{10,9... | collective-permute-start | bytes 1572872 | tf_op jit(solution)/shard_map/ppermute | solution.py:311
  207.3 13.8 %collective-permute-start.15 = (bf16[256,1024]{1,0:T(8,128)(2,1)S(1)}, bf16[256,1024]{1,0:T(8,128)(2,1)S(1)}, u32[]{:S(2)}, u32[]{:S(2)}) collective-permute-start(bf16[256,1024]{1,0:T(8,128)(2,1)S(1)} %get-tuple-element.23), channel_id=1, source_target_pairs={{0,2},{1,3},{2,0},{3,1},{4,6},{5,7},{6,4},{7,5},{8,10},{9,11},{10,... | collective-permute-start | bytes 1572872 | tf_op jit(solution)/shard_map/ppermute | solution.py:311
  (17 other events, 68.6 us)
